TPU v7x, 32 devices: a whole 2x2x4 slice. The times are simulated.
32 devices in a mesh: freq: 8 (over z, x), unk: 4 (over y, core).
Axes of the slice: x: 2, y: 2, z: 4, core: 2. Of those that a mesh axis runs over, the one named last changes fastest.
Arguments:
- time_samples: bfloat16 [16, 32, 2048], P(None, 'freq', 'unk'), may hold values from -3 to 3
- inverse_offset: bfloat16 [2, 8, 2048, 512], P(None, 'freq', 'unk'), may hold values from -0.09375 to 0.09375
- coupling_near: bfloat16 [2, 8, 2048, 512], P(None, 'freq', 'unk'), may hold values from -0.125 to 0.125
- coupling_far: bfloat16 [2, 8, 2048, 512], P(None, 'freq', 'unk'), may hold values from -0.09375 to 0.09375
Outputs:
- solution: bfloat16 [2, 8, 32, 2048], P(None, 'freq', None, 'unk')
All inputs are finite; a program needn't handle non-finite values.
Results may differ from a plain program's by a relative error of at most 0.017.
Values may be sent and summed in bfloat16 or wider, within the bound.
A program may use at most 64 MiB of HBM per device.

v0:
```python
import functools
import math

import jax
import jax.numpy as jnp
import numpy as np
from jax import lax
from jax.experimental import pallas as pl
from jax.experimental.pallas import tpu as pltpu
from jax.sharding import PartitionSpec as P

MESH = pl.DeviceIdType.MESH


def transform_matrix(times, freqs, loads):
    moment = np.arange(times)
    angle = (np.arange(freqs)[:, None] * moment[None, :] % times) * (2.0 * math.pi / times)
    damping = np.power(0.5, moment / times) / math.sqrt(times)
    table = np.stack([damping * np.cos(angle), -damping * np.sin(angle)], axis=1)
    full = np.einsum("kct,lm->kcltm", table, np.eye(loads)).astype(np.float32)
    full = full.reshape(freqs * 2 * loads, times * loads)
    high = full.astype(jnp.bfloat16)
    rest = (full - high.astype(np.float32)).astype(jnp.bfloat16)
    return np.concatenate([high, rest], axis=1)


def dot(left, right):
    return jnp.dot(left, right, preferred_element_type=jnp.float32)


def widened(value):
    half = value.shape[0] // 2
    real, imag = value[:half], value[half:]
    return jnp.concatenate(
        [jnp.concatenate([real, -imag], axis=1), jnp.concatenate([imag, real], axis=1)], axis=0
    )


def kernel(
    n_freq, n_unk, chunk,
    ts_hbm, w_hbm, o_hbm, c_hbm, f_hbm, out_ref,
    ts, w, o, c, f, near, far, sp, rb, xb, xin, acc, first_o, first_rb,
    load_sem, send_sem, recv_sem, xsend_sem, xrecv_sem, first_send_sem, first_recv_sem, share_sem,
):
    me = lax.axis_index("freq")
    pos = lax.axis_index("unk")
    loads = ts.shape[1]
    rows = o.shape[1]

    copies = [
        pltpu.make_async_copy(src, dst, load_sem.at[i])
        for i, (src, dst) in enumerate(
            [(ts_hbm, ts), (w_hbm, w), (o_hbm.at[:, 0], o), (c_hbm.at[:, 0], c), (f_hbm.at[:, 0], f)]
        )
    ]
    for copy in copies[:2]:
        copy.start()

    barrier = pltpu.get_barrier_semaphore()
    for d in range(1, n_freq):
        pl.semaphore_signal(
            barrier, inc=1, device_id={"freq": lax.rem(me + d, n_freq)}, device_id_type=MESH
        )
    for d in (1, 2):
        @pl.when(pos + d < n_unk)
        def _():
            pl.semaphore_signal(barrier, inc=1, device_id={"unk": pos + d}, device_id_type=MESH)

        @pl.when(pos >= d)
        def _():
            pl.semaphore_signal(barrier, inc=1, device_id={"unk": pos - d}, device_id_type=MESH)

    @pl.when(pos == 1)
    def _():
        for d in range(1, n_freq):
            pl.semaphore_signal(
                barrier, inc=1,
                device_id={"freq": lax.rem(me + d, n_freq), "unk": 0}, device_id_type=MESH,
            )

    for copy in copies[2:]:
        copy.start()

    copies[0].wait()
    copies[1].wait()
    samples = ts[...].astype(jnp.float32).reshape(-1, rows).astype(jnp.bfloat16)
    spectra = dot(w[...], jnp.concatenate([samples, samples], axis=0))
    sp[...] = spectra.reshape(sp.shape).astype(jnp.bfloat16)

    def reduce_block(src, dst):
        def part(i):
            at = pl.ds(pl.multiple_of(i * chunk, chunk), chunk)
            real, imag = src[0, at, :], src[1, at, :]
            weights = o[...].reshape(2 * rows, rows)
            new_real = dot(jnp.concatenate([real, -imag], axis=1), weights)
            dst[0, at, :] = (real.astype(jnp.float32) + new_real).astype(jnp.bfloat16)
            new_imag = dot(jnp.concatenate([imag, real], axis=1), weights)
            dst[1, at, :] = (imag.astype(jnp.float32) + new_imag).astype(jnp.bfloat16)

        pl.loop(0, rows // chunk)(part)

    pl.semaphore_wait(
        barrier,
        (n_freq - 1) * (1 + (pos == 0).astype(jnp.int32))
        + sum(
            (pos + d < n_unk).astype(jnp.int32) + (pos >= d).astype(jnp.int32) for d in (1, 2)
        ),
    )

    def share_offset():
        return pltpu.make_async_remote_copy(
            src_ref=o_hbm.at[:, 0], dst_ref=first_o,
            send_sem=share_sem.at[0], recv_sem=share_sem.at[1],
            device_id={"unk": 1}, device_id_type=MESH,
        )

    def share_spectra(target, source, at):
        return pltpu.make_async_remote_copy(
            src_ref=sp.at[target], dst_ref=first_rb.at[source],
            send_sem=first_send_sem.at[at], recv_sem=first_recv_sem.at[source],
            device_id={"freq": target, "unk": 1}, device_id_type=MESH,
        )

    def other(d):
        upper = (me * 2) // n_freq
        rising = (d - 1) + (d - 1 >= me).astype(jnp.int32)
        falling = (n_freq - d) - (n_freq - d <= me).astype(jnp.int32)
        return upper * rising + (1 - upper) * falling

    @pl.when(pos == 0)
    def _():
        for d in range(1, n_freq):
            share_spectra(other(d), me, d).start()
        share_spectra(me, me, 0).start()
        share_offset().start()

    sends = []
    for d in range(1, n_freq):
        target = other(d)
        send = pltpu.make_async_remote_copy(
            src_ref=sp.at[target], dst_ref=rb.at[me],
            send_sem=send_sem.at[d], recv_sem=recv_sem.at[me],
            device_id={"freq": target}, device_id_type=MESH,
        )
        send.start()
        sends.append(send)
    rb[me] = sp[me]

    copies[2].wait()
    copies[3].wait()
    copies[4].wait()

    @pl.when(pos >= 1)
    def _():
        reduce_block(c, near)

    @pl.when(pos >= 2)
    def _():
        reduce_block(f, far)

    for d in range(1, n_freq):
        source = lax.rem(me + n_freq - d, n_freq)
        pltpu.make_async_remote_copy(
            src_ref=rb.at[source], dst_ref=rb.at[source],
            send_sem=send_sem.at[d], recv_sem=recv_sem.at[source],
            device_id={"freq": source}, device_id_type=MESH,
        ).wait_recv()

    odd = lax.rem(pos, 2) == 1
    ahead = lax.rem(pos + 1, n_unk)

    def to_next(slot, src, sem):
        return pltpu.make_async_remote_copy(
            src_ref=src, dst_ref=xin.at[slot],
            send_sem=xsend_sem.at[sem], recv_sem=xrecv_sem.at[slot],
            device_id={"unk": ahead}, device_id_type=MESH,
        )

    def to_second():
        return pltpu.make_async_remote_copy(
            src_ref=xb, dst_ref=xin.at[1],
            send_sem=xsend_sem.at[1], recv_sem=xrecv_sem.at[1],
            device_id={"unk": lax.rem(pos + 2, n_unk)}, device_id_type=MESH,
        )

    def drive(spectra_in, offset):
        got = spectra_in[...].astype(jnp.float32)
        got = jnp.concatenate(
            [got[:, :loads].reshape(-1, rows), got[:, loads:].reshape(-1, rows)], axis=0
        )
        return got + dot(widened(got.astype(jnp.bfloat16)), offset[...].reshape(2 * rows, rows))

    acc[...] = drive(rb, o)

    @pl.when(pos == 1)
    def _():
        for d in range(n_freq):
            source = lax.rem(me + n_freq - d, n_freq)
            share_spectra(source, source, d).wait_recv()
        share_offset().wait_recv()
        first = drive(first_rb, first_o).astype(jnp.bfloat16)
        xin[0] = first

        @pl.when(pos + 1 < n_unk)
        def _():
            to_next(1, xin.at[0], 2).start()

        acc[...] -= dot(widened(first), near[...].reshape(2 * rows, rows))


    has_next = jnp.logical_and(pos >= 1, pos + 1 < n_unk)
    has_second = jnp.logical_and(jnp.logical_and(pos >= 2, pos + 2 < n_unk), jnp.logical_not(odd))
    hands_on = jnp.logical_and(jnp.logical_and(pos >= 2, has_next), jnp.logical_not(odd))

    @pl.when(pos >= 2)
    def _():
        @pl.when(jnp.logical_not(odd))
        def _():
            to_second().wait_recv()

        @pl.when(odd)
        def _():
            to_next(1, xin.at[0], 2).wait_recv()

        acc[...] -= dot(widened(xin[1]), far[...].reshape(2 * rows, rows))

    @pl.when(pos >= 2)
    def _():
        to_next(0, xb, 0).wait_recv()

        @pl.when(hands_on)
        def _():
            to_next(1, xin.at[0], 2).start()

        acc[...] -= dot(widened(xin[0]), near[...].reshape(2 * rows, rows))

    solved = acc[...].astype(jnp.bfloat16)
    xb[...] = solved
    out_ref[...] = solved.reshape(out_ref.shape)

    @pl.when(has_next)
    def _():
        to_next(0, xb, 0).start()

    @pl.when(has_second)
    def _():
        to_second().start()


    for send in sends:
        send.wait_send()

    @pl.when(pos == 0)
    def _():
        for d in range(n_freq):
            share_spectra(me, me, d).wait_send()
        share_offset().wait_send()

    @pl.when(jnp.logical_or(hands_on, jnp.logical_and(pos == 1, has_next)))
    def _():
        to_next(1, xin.at[0], 2).wait_send()

    @pl.when(has_next)
    def _():
        to_next(0, xb, 0).wait_send()

    @pl.when(has_second)
    def _():
        to_second().wait_send()


def per_device(n_freq, n_unk, time_samples, inverse_offset, coupling_near, coupling_far):
    times, loads, rows = time_samples.shape
    freqs = inverse_offset.shape[1] * n_freq
    table = jnp.asarray(transform_matrix(times, freqs, loads))
    block = (2, rows, rows)
    wide = 2 * n_freq * loads
    bf16 = jnp.bfloat16
    return pl.pallas_call(
        functools.partial(kernel, n_freq, n_unk, min(256, rows)),
        out_shape=pltpu.VMEM((2, 1, n_freq * loads, rows), bf16),
        in_specs=[pl.BlockSpec(memory_space=pl.ANY)] * 5,
        out_specs=pl.BlockSpec(memory_space=pltpu.VMEM),
        scratch_shapes=[
            pltpu.VMEM(time_samples.shape, bf16),
            pltpu.VMEM(table.shape, bf16),
            pltpu.VMEM(block, bf16),
            pltpu.VMEM(block, bf16),
            pltpu.VMEM(block, bf16),
            pltpu.VMEM(block, bf16),
            pltpu.VMEM(block, bf16),
            pltpu.VMEM((n_freq, 2 * loads, rows), bf16),
            pltpu.VMEM((n_freq, 2 * loads, rows), bf16),
            pltpu.VMEM((wide, rows), bf16),
            pltpu.VMEM((2, wide, rows), bf16),
            pltpu.VMEM((wide, rows), jnp.float32),
            pltpu.VMEM(block, bf16),
            pltpu.VMEM((n_freq, 2 * loads, rows), bf16),
            pltpu.SemaphoreType.DMA((5,)),
            pltpu.SemaphoreType.DMA((n_freq,)),
            pltpu.SemaphoreType.DMA((n_freq,)),
            pltpu.SemaphoreType.DMA((3,)),
            pltpu.SemaphoreType.DMA((2,)),
            pltpu.SemaphoreType.DMA((n_freq,)),
            pltpu.SemaphoreType.DMA((n_freq,)),
            pltpu.SemaphoreType.DMA((2,)),
        ],
        compiler_params=pltpu.CompilerParams(collective_id=0, has_side_effects=True),
    )(time_samples, table, inverse_offset, coupling_near, coupling_far)


def solution(mesh):
    placed = (
        P(None, "freq", "unk"),
        P(None, "freq", "unk", None),
        P(None, "freq", "unk", None),
        P(None, "freq", "unk", None),
    )
    return jax.shard_map(
        functools.partial(per_device, mesh.shape["freq"], mesh.shape["unk"]),
        mesh=mesh,
        in_specs=placed,
        out_specs=P(None, "freq", None, "unk"),
        check_vma=False,
    )
```

profile of v0, /device:TPU:5, one launch (start us, length us, event | category | flops | bytes accessed | tf_op | source)
XLA Modules:
  0.0 13.7 jit_solution(8928791477344935893)
XLA Ops:
  0.0 13.0 %shard_map.55 = bf16[2,1,32,512]{3,2,1,0:T(8,128)(2,1)S(1)} custom-call(bf16[16,4,512]{2,1,0:T(4,128)(2,1)} %ts_hbm.1, bf16[64,128]{1,0:T(8,128)(2,1)} %constant.2.clone.w_hbm, bf16[2,1,512,512]{3,2,1,0:T(8,128)(2,1)} %o_hbm.1, bf16[2,1,512,512]{3,2,1,0:T(8,128)(2,1)} %c_hbm.1, bf16[2,1,512,512]{3,2,1,0:T(8,128)(2,1)} %f_hbm.1), custom_call_target="tpu_custom_call" | custom-call | tf_op jit(solution)/shard_map/pallas_call | solution.py:279
  13.1 0.6 %copy.7 = bf16[2,1,32,512]{3,2,1,0:T(8,128)(2,1)} copy(bf16[2,1,32,512]{3,2,1,0:T(8,128)(2,1)S(1)} %shard_map.55) | data formatting | bytes 131072
where the time goes:
time: 13.8 us; the launch traced here: 13.7 us
  Pallas kernels  13 us (94%)
  local copies, waits for them, and re-layouts  0.63 us (5%)
    pallas_call x1, Pallas kernels, per_device(): pl.pallas_call(functools.partial(kernel, n_freq, n_unk, min(256, rows)),...  13 us
    unnamed x1, local copies, waits for them, and re-layouts  0.63 us

commit v1 on v0

v1 whole, which is shorter than its diff:
```python
import functools
import math

import jax
import jax.numpy as jnp
import numpy as np
from jax import lax
from jax.experimental import pallas as pl
from jax.experimental.pallas import tpu as pltpu
from jax.sharding import PartitionSpec as P

MESH = pl.DeviceIdType.MESH


def transform_matrix(times, freqs, loads):
    moment = np.arange(times)
    angle = (np.arange(freqs)[:, None] * moment[None, :] % times) * (2.0 * math.pi / times)
    damping = np.power(0.5, moment / times) / math.sqrt(times)
    table = np.stack([damping * np.cos(angle), -damping * np.sin(angle)], axis=1)
    full = np.einsum("kct,lm->kcltm", table, np.eye(loads)).astype(np.float32)
    full = full.reshape(freqs * 2 * loads, times * loads)
    high = full.astype(jnp.bfloat16)
    rest = (full - high.astype(np.float32)).astype(jnp.bfloat16)
    return np.concatenate([high, rest], axis=1)


def dot(left, right):
    return jnp.dot(left, right, preferred_element_type=jnp.float32)


def kernel(
    n_freq, n_unk, chunk,
    ts_hbm, w_hbm, o_hbm, c_hbm, f_hbm, out_ref,
    ts, w, o, c, f, near, far, mixed, o_even, c_even, f_even,
    sp, rb_even, rb_odd, xs, xin, acc,
    load_sem, send_sem, recv_sem, share_send, share_recv, pass_send, pass_recv,
    hop_send, hop_recv, hand_send, hand_recv, ready,
):
    me = lax.axis_index("freq")
    pos = lax.axis_index("unk")
    loads = ts.shape[1]
    rows = o.shape[1]
    slot_rows = 2 * loads
    n_far = max(1, n_freq // 4)
    n_near = n_freq - n_far
    is_odd = lax.rem(pos, 2) == 1
    is_even = jnp.logical_not(is_odd)
    partner = pos + 1 - 2 * lax.rem(pos, 2)
    first_pair = pos < 2
    later_pair = pos >= 2
    has_next = pos + 2 < n_unk
    near_slots, far_slots = pl.ds(0, n_near), pl.ds(n_near, n_far)
    groups = (near_slots, far_slots)

    def upper(freq):
        return (freq * 2) // n_freq

    def slot_of(source, target):
        return lax.rem(source + n_freq - n_far * upper(target), n_freq)

    def remote(src, dst, send, recv, unk, freq=me):
        return pltpu.make_async_remote_copy(
            src_ref=src, dst_ref=dst, send_sem=send, recv_sem=recv,
            device_id={"freq": freq, "unk": unk}, device_id_type=MESH,
        )

    loaded = [
        pltpu.make_async_copy(src, dst, load_sem.at[i])
        for i, (src, dst) in enumerate(
            [(ts_hbm, ts), (w_hbm, w), (o_hbm.at[:, 0], o), (c_hbm.at[:, 0], c), (f_hbm.at[:, 0], f)]
        )
    ]
    loaded[0].start()
    loaded[1].start()

    barrier = pltpu.get_barrier_semaphore()

    def greet(freq, unk):
        pl.semaphore_signal(
            barrier, inc=1, device_id={"freq": freq, "unk": unk}, device_id_type=MESH
        )

    def other(d):
        rising = (d - 1) + (d - 1 >= me).astype(jnp.int32)
        falling = (n_freq - d) - (n_freq - d <= me).astype(jnp.int32)
        return upper(me) * rising + (1 - upper(me)) * falling

    @pl.when(is_odd)
    def _():
        for d in range(1, n_freq):
            greet(other(d), pos)

        @pl.when(later_pair)
        def _():
            greet(me, pos - 2)

    greet(me, partner)
    loaded[2].start()

    @pl.when(pos >= 1)
    def _():
        loaded[3].start()

    @pl.when(later_pair)
    def _():
        loaded[4].start()

    def share(i):
        src = (o_hbm, c_hbm, f_hbm)[i]
        dst = (o_even, c_even, f_even)[i]
        return remote(src.at[:, 0], dst, share_send.at[i], share_recv.at[i], partner)

    @pl.when(is_even)
    def _():
        pl.semaphore_wait(barrier, 1)
        share(0).start()

    loaded[0].wait()
    loaded[1].wait()
    samples = ts[...].astype(jnp.float32).reshape(-1, rows).astype(jnp.bfloat16)
    spectra = dot(w[...], jnp.concatenate([samples, samples], axis=0))
    sp[...] = spectra.reshape(sp.shape).astype(jnp.bfloat16)

    def spread(kind, target):
        slot = slot_of(me, target)
        group = (slot >= n_near).astype(jnp.int32)
        return remote(
            sp.at[target], (rb_even, rb_odd)[kind].at[slot],
            send_sem.at[0], recv_sem.at[2 * kind + group], pos + 1 - kind, target,
        )

    def product(base, left, weights, dst):
        def part(i):
            at = pl.ds(pl.multiple_of(i * chunk, chunk), chunk)
            real, imag = left[0, at, :], left[1, at, :]
            both = weights[...].reshape(2 * rows, rows)
            new_real = dot(jnp.concatenate([real, -imag], axis=1), both)
            dst[0, at, :] = (base[0, at, :].astype(jnp.float32) + new_real).astype(jnp.bfloat16)
            new_imag = dot(jnp.concatenate([imag, real], axis=1), both)
            dst[1, at, :] = (base[1, at, :].astype(jnp.float32) + new_imag).astype(jnp.bfloat16)

        pl.loop(0, rows // chunk)(part)

    def times(x, weights):
        direct = dot(x, weights[0])
        turned = dot(x, weights[1]).reshape(-1, slot_rows, rows)
        turned = jnp.concatenate([-turned[:, loads:], turned[:, :loads]], axis=1)
        return direct + turned.reshape(-1, rows)

    def flat(value):
        wide = value.astype(jnp.float32).reshape(-1, rows)
        return wide, wide.astype(jnp.bfloat16)

    def slots(value):
        return value.reshape(-1, slot_rows, rows)

    def emit(value):
        value = slots(value)

        def put(ordered):
            for part in range(2):
                at = slice(part * loads, (part + 1) * loads)
                out_ref[part, 0] = ordered[:, at].reshape(-1, rows).astype(jnp.bfloat16)

        @pl.when(upper(me) == 0)
        def _():
            put(value)

        @pl.when(upper(me) == 1)
        def _():
            put(jnp.concatenate([value[n_near:], value[:n_near]], axis=0))

    def pass_on(i):
        at = groups[i]
        return remote(rb_even.at[at], rb_even.at[at], pass_send.at[i], pass_recv.at[i], partner)

    def hop(i):
        at = groups[i]
        return remote(xs.at[:, at], xin.at[:, at], hop_send.at[i], hop_recv.at[i], lax.rem(pos + 2, n_unk))

    def hand_on(i):
        at = groups[i]
        return remote(xin.at[:, at], xin.at[:, at], hand_send.at[i], hand_recv.at[i], partner)

    def received(kind, group):
        count = n_far if group else n_near - kind
        at = pl.ds(n_near if group else 0, count)
        ref = (rb_even, rb_odd)[kind].at[at]
        remote(ref, ref, send_sem.at[0], recv_sem.at[2 * kind + group], partner).wait_recv()

    @pl.when(is_odd)
    def _():
        pl.semaphore_wait(barrier, n_freq + has_next.astype(jnp.int32))
        pl.semaphore_signal(
            ready, inc=1, device_id={"freq": me, "unk": partner}, device_id_type=MESH
        )
        for d in range(1, n_freq):
            spread(1, other(d)).start()
        rb_odd[slot_of(me, me)] = sp[me]

        loaded[2].wait()
        loaded[3].wait()
        product(c, c, o, near)

        @pl.when(later_pair)
        def _():
            loaded[4].wait()
            product(f, f, o, far)

        share(0).wait_recv()
        product(near, o_even, near, mixed)

        @pl.when(first_pair)
        def _():
            for i, (low, high) in enumerate([(0, n_near), (n_near, n_freq)]):
                received(1, i)
                wide, tight = flat(rb_odd[low:high])
                driven = wide + times(tight, o)
                received(0, i)
                pass_on(i).start()
                wide, tight = flat(rb_even[low:high])
                xs[0, low:high] = slots(wide + times(tight, o_even)).astype(jnp.bfloat16)
                solved = slots(driven - times(tight, mixed))
                xs[1, low:high] = solved.astype(jnp.bfloat16)
                acc[low:high] = solved

                @pl.when(has_next)
                def _():
                    hop(i).start()

            emit(acc[...])

        @pl.when(later_pair)
        def _():
            for i in range(2):
                received(1, i)
                received(0, i)
                pass_on(i).start()
            wide, tight = flat(rb_odd[...])
            acc[...] = slots(wide + times(tight, o))
            share(1).wait_recv()
            share(2).wait_recv()
            for i in range(2):
                hop(i).wait_recv()
                hand_on(i).start()
            before = flat(xin[0])[1]
            last = flat(xin[1])[1]
            rest = flat(rb_even[...])[0] - times(last, c_even) - times(before, f_even)
            tight = rest.astype(jnp.bfloat16)
            solved = acc[...].reshape(-1, rows) - times(last, far) - times(tight, mixed)
            if n_unk > 4:
                @pl.when(has_next)
                def _():
                    xs[0] = slots(rest + times(tight, o_even)).astype(jnp.bfloat16)
                    xs[1] = slots(solved).astype(jnp.bfloat16)
                    hop(0).start()
                    hop(1).start()
            emit(solved)
            for i in range(2):
                hand_on(i).wait_send()

        for i in range(2):
            pass_on(i).wait_send()
        sent = sp.at[pl.ds(0, n_freq - 1)]
        remote(sent, sent, send_sem.at[0], recv_sem.at[0], partner).wait_send()

        @pl.when(has_next)
        def _():
            for i in range(2):
                hop(i).wait_send()

    @pl.when(is_even)
    def _():
        pl.semaphore_wait(ready, 1)
        for d in range(1, n_freq):
            spread(0, other(d)).start()
        spread(0, me).start()

        @pl.when(later_pair)
        def _():
            share(1).start()
            share(2).start()

        loaded[2].wait()

        @pl.when(later_pair)
        def _():
            loaded[3].wait()
            product(c, c, o, near)
            loaded[4].wait()
            product(f, f, o, far)

        for i in range(2):
            pass_on(i).wait_recv()
        wide, tight = flat(rb_even[...])
        acc[...] = slots(wide + times(tight, o))

        @pl.when(later_pair)
        def _():
            for i in range(2):
                hand_on(i).wait_recv()
            acc[...] -= slots(times(flat(xin[1])[1], near) + times(flat(xin[0])[1], far))

        emit(acc[...])
        share(0).wait_send()

        @pl.when(later_pair)
        def _():
            share(1).wait_send()
            share(2).wait_send()

        remote(sp, sp, send_sem.at[0], recv_sem.at[0], partner).wait_send()


def per_device(n_freq, n_unk, time_samples, inverse_offset, coupling_near, coupling_far):
    times, loads, rows = time_samples.shape
    freqs = inverse_offset.shape[1] * n_freq
    table = jnp.asarray(transform_matrix(times, freqs, loads))
    bf16 = jnp.bfloat16
    block = pltpu.VMEM((2, rows, rows), bf16)
    wide = (n_freq, 2 * loads, rows)
    dma = pltpu.SemaphoreType.DMA
    return pl.pallas_call(
        functools.partial(kernel, n_freq, n_unk, min(256, rows)),
        out_shape=pltpu.VMEM((2, 1, n_freq * loads, rows), bf16),
        in_specs=[pl.BlockSpec(memory_space=pl.ANY)] * 5,
        out_specs=pl.BlockSpec(memory_space=pltpu.VMEM),
        scratch_shapes=[
            pltpu.VMEM(time_samples.shape, bf16),
            pltpu.VMEM(table.shape, bf16),
            *[block] * 9,
            pltpu.VMEM(wide, bf16),
            pltpu.VMEM(wide, bf16),
            pltpu.VMEM(wide, bf16),
            pltpu.VMEM((2, *wide), bf16),
            pltpu.VMEM((2, *wide), bf16),
            pltpu.VMEM(wide, jnp.float32),
            dma((5,)), dma((1,)), dma((4,)), dma((3,)), dma((3,)),
            dma((2,)), dma((2,)), dma((2,)), dma((2,)), dma((2,)), dma((2,)),
            pltpu.SemaphoreType.REGULAR,
        ],
        compiler_params=pltpu.CompilerParams(collective_id=0, has_side_effects=True),
    )(time_samples, table, inverse_offset, coupling_near, coupling_far)


def solution(mesh):
    placed = (
        P(None, "freq", "unk"),
        P(None, "freq", "unk", None),
        P(None, "freq", "unk", None),
        P(None, "freq", "unk", None),
    )
    return jax.shard_map(
        functools.partial(per_device, mesh.shape["freq"], mesh.shape["unk"]),
        mesh=mesh,
        in_specs=placed,
        out_specs=P(None, "freq", None, "unk"),
        check_vma=False,
    )
```

time: 13.8 us -> 12.5 us (0.906)
  the two profiles are of different devices: /device:TPU:5 before, /device:TPU:4 now
where the time goes in v1:
time: 12.5 us; the launch traced here: 12.4 us
  Pallas kernels  11.7 us (94%)
  local copies, waits for them, and re-layouts  0.63 us (5%)
    pallas_call x1, Pallas kernels, per_device(): pl.pallas_call(functools.partial(kernel, n_freq, n_unk, min(256, rows)),...  11.7 us
    unnamed x1, local copies, waits for them, and re-layouts  0.63 us

profile of v1, /device:TPU:4, one launch (start us, length us, event | category | flops | bytes accessed | tf_op | source)
XLA Modules:
  0.0 12.4 jit_solution(7065539503166532211)
XLA Ops:
  0.0 11.7 %shard_map.55 = bf16[2,1,32,512]{3,2,1,0:T(8,128)(2,1)S(1)} custom-call(bf16[16,4,512]{2,1,0:T(4,128)(2,1)} %ts_hbm.1, bf16[64,128]{1,0:T(8,128)(2,1)} %constant.2.clone.w_hbm, bf16[2,1,512,512]{3,2,1,0:T(8,128)(2,1)} %o_hbm.1, bf16[2,1,512,512]{3,2,1,0:T(8,128)(2,1)} %c_hbm.1, bf16[2,1,512,512]{3,2,1,0:T(8,128)(2,1)} %f_hbm.1), custom_call_target="tpu_custom_call" | custom-call | tf_op jit(solution)/shard_map/pallas_call | solution.py:323
  11.8 0.6 %copy.7 = bf16[2,1,32,512]{3,2,1,0:T(8,128)(2,1)} copy(bf16[2,1,32,512]{3,2,1,0:T(8,128)(2,1)S(1)} %shard_map.55) | data formatting | bytes 131072

commit v2 on v1

--- a/solution.py
+++ b/solution.py
@@ -29,10 +29,10 @@
 
 
 def kernel(
-    n_freq, n_unk, chunk,
+    n_freq, n_unk, n_far, chunk,
     ts_hbm, w_hbm, o_hbm, c_hbm, f_hbm, out_ref,
     ts, w, o, c, f, near, far, mixed, o_even, c_even, f_even,
-    sp, rb_even, rb_odd, xs, xin, acc,
+    sp, rb_even, rb_odd, xs, xs_far, xin, xin_far, acc, tail,
     load_sem, send_sem, recv_sem, share_send, share_recv, pass_send, pass_recv,
     hop_send, hop_recv, hand_send, hand_recv, ready,
 ):
@@ -40,8 +40,6 @@
     pos = lax.axis_index("unk")
     loads = ts.shape[1]
     rows = o.shape[1]
-    slot_rows = 2 * loads
-    n_far = max(1, n_freq // 4)
     n_near = n_freq - n_far
     is_odd = lax.rem(pos, 2) == 1
     is_even = jnp.logical_not(is_odd)
@@ -49,8 +47,9 @@
     first_pair = pos < 2
     later_pair = pos >= 2
     has_next = pos + 2 < n_unk
-    near_slots, far_slots = pl.ds(0, n_near), pl.ds(n_near, n_far)
-    groups = (near_slots, far_slots)
+    quarter = (me * 4) // n_freq
+    bounds = ((0, n_near), (n_near, n_freq))
+    x_out, x_in, kept = (xs, xs_far), (xin, xin_far), (acc, tail)
 
     def upper(freq):
         return (freq * 2) // n_freq
@@ -112,8 +111,17 @@
 
     @pl.when(is_even)
     def _():
+        @pl.when(later_pair)
+        def _():
+            greet(me, pos - 1)
+
         pl.semaphore_wait(barrier, 1)
         share(0).start()
+
+        @pl.when(later_pair)
+        def _():
+            share(1).start()
+            share(2).start()
 
     loaded[0].wait()
     loaded[1].wait()
@@ -141,46 +149,55 @@
 
         pl.loop(0, rows // chunk)(part)
 
+    def near_product():
+        loaded[2].wait()
+        loaded[3].wait()
+        product(c, c, o, near)
+
+    def far_product():
+        loaded[4].wait()
+        product(f, f, o, far)
+
+    def mixed_product():
+        share(0).wait_recv()
+        product(near, o_even, near, mixed)
+
     def times(x, weights):
         direct = dot(x, weights[0])
-        turned = dot(x, weights[1]).reshape(-1, slot_rows, rows)
-        turned = jnp.concatenate([-turned[:, loads:], turned[:, :loads]], axis=1)
-        return direct + turned.reshape(-1, rows)
-
-    def flat(value):
-        wide = value.astype(jnp.float32).reshape(-1, rows)
-        return wide, wide.astype(jnp.bfloat16)
-
-    def slots(value):
-        return value.reshape(-1, slot_rows, rows)
-
-    def emit(value):
-        value = slots(value)
-
-        def put(ordered):
-            for part in range(2):
-                at = slice(part * loads, (part + 1) * loads)
-                out_ref[part, 0] = ordered[:, at].reshape(-1, rows).astype(jnp.bfloat16)
-
-        @pl.when(upper(me) == 0)
-        def _():
-            put(value)
-
-        @pl.when(upper(me) == 1)
-        def _():
-            put(jnp.concatenate([value[n_near:], value[:n_near]], axis=0))
+        turned = dot(x, weights[1])
+        half = x.shape[0] // 2
+        return direct + jnp.concatenate([-turned[half:], turned[:half]], axis=0)
+
+    def ordered(ref, group):
+        low, high = bounds[group]
+        value = ref[low:high].astype(jnp.float32)
+        value = jnp.concatenate(
+            [value[:, :loads].reshape(-1, rows), value[:, loads:].reshape(-1, rows)], axis=0
+        )
+        return value, value.astype(jnp.bfloat16)
+
+    def emit(close, distant):
+        swapped = upper(me) == 1
+        for part in range(2):
+            a = close[part * n_near * loads:(part + 1) * n_near * loads]
+            b = distant[part * n_far * loads:(part + 1) * n_far * loads]
+            value = jnp.where(
+                swapped, jnp.concatenate([b, a], axis=0), jnp.concatenate([a, b], axis=0)
+            )
+            out_ref[part, 0] = value.astype(jnp.bfloat16)
 
     def pass_on(i):
-        at = groups[i]
+        at = pl.ds(bounds[i][0], bounds[i][1] - bounds[i][0])
         return remote(rb_even.at[at], rb_even.at[at], pass_send.at[i], pass_recv.at[i], partner)
 
     def hop(i):
-        at = groups[i]
-        return remote(xs.at[:, at], xin.at[:, at], hop_send.at[i], hop_recv.at[i], lax.rem(pos + 2, n_unk))
-
-    def hand_on(i):
-        at = groups[i]
-        return remote(xin.at[:, at], xin.at[:, at], hand_send.at[i], hand_recv.at[i], partner)
+        return remote(x_out[i], x_in[i], hop_send.at[i], hop_recv.at[i], lax.rem(pos + 2, n_unk))
+
+    def hop_even():
+        return remote(xs_far, xin_far, hop_send.at[2], hop_recv.at[2], lax.rem(pos + 1, n_unk))
+
+    def hand_on():
+        return remote(xin, xin, hand_send.at[0], hand_recv.at[0], partner)
 
     def received(kind, group):
         count = n_far if group else n_near - kind
@@ -190,7 +207,21 @@
 
     @pl.when(is_odd)
     def _():
-        pl.semaphore_wait(barrier, n_freq + has_next.astype(jnp.int32))
+        @pl.when(quarter < 2)
+        def _():
+            near_product()
+
+        @pl.when(quarter == 0)
+        def _():
+            @pl.when(first_pair)
+            def _():
+                mixed_product()
+
+            @pl.when(later_pair)
+            def _():
+                far_product()
+
+        pl.semaphore_wait(barrier, n_freq + 2 * has_next.astype(jnp.int32))
         pl.semaphore_signal(
             ready, inc=1, device_id={"freq": me, "unk": partner}, device_id_type=MESH
         )
@@ -198,37 +229,39 @@
             spread(1, other(d)).start()
         rb_odd[slot_of(me, me)] = sp[me]
 
-        loaded[2].wait()
-        loaded[3].wait()
-        product(c, c, o, near)
-
-        @pl.when(later_pair)
-        def _():
-            loaded[4].wait()
-            product(f, f, o, far)
-
-        share(0).wait_recv()
-        product(near, o_even, near, mixed)
+        @pl.when(quarter >= 2)
+        def _():
+            near_product()
+
+        @pl.when(jnp.logical_and(quarter >= 1, later_pair))
+        def _():
+            far_product()
+
+        @pl.when(jnp.logical_or(quarter >= 1, later_pair))
+        def _():
+            mixed_product()
 
         @pl.when(first_pair)
         def _():
-            for i, (low, high) in enumerate([(0, n_near), (n_near, n_freq)]):
+            for i in range(2):
                 received(1, i)
-                wide, tight = flat(rb_odd[low:high])
+                wide, tight = ordered(rb_odd, i)
                 driven = wide + times(tight, o)
                 received(0, i)
                 pass_on(i).start()
-                wide, tight = flat(rb_even[low:high])
-                xs[0, low:high] = slots(wide + times(tight, o_even)).astype(jnp.bfloat16)
-                solved = slots(driven - times(tight, mixed))
-                xs[1, low:high] = solved.astype(jnp.bfloat16)
-                acc[low:high] = solved
+                wide, tight = ordered(rb_even, i)
+                x_out[i][0] = (wide + times(tight, o_even)).astype(jnp.bfloat16)
+                solved = driven - times(tight, mixed)
+                x_out[i][1] = solved.astype(jnp.bfloat16)
+                kept[i][...] = solved
 
                 @pl.when(has_next)
                 def _():
                     hop(i).start()
-
-            emit(acc[...])
+                    if i == 1:
+                        hop_even().start()
+
+            emit(acc[...], tail[...])
 
         @pl.when(later_pair)
         def _():
@@ -236,28 +269,32 @@
                 received(1, i)
                 received(0, i)
                 pass_on(i).start()
-            wide, tight = flat(rb_odd[...])
-            acc[...] = slots(wide + times(tight, o))
+            for i in range(2):
+                wide, tight = ordered(rb_odd, i)
+                kept[i][...] = wide + times(tight, o)
             share(1).wait_recv()
             share(2).wait_recv()
-            for i in range(2):
+            done = []
+            for i in range(2):
+                rest = ordered(rb_even, i)[0]
                 hop(i).wait_recv()
-                hand_on(i).start()
-            before = flat(xin[0])[1]
-            last = flat(xin[1])[1]
-            rest = flat(rb_even[...])[0] - times(last, c_even) - times(before, f_even)
-            tight = rest.astype(jnp.bfloat16)
-            solved = acc[...].reshape(-1, rows) - times(last, far) - times(tight, mixed)
-            if n_unk > 4:
-                @pl.when(has_next)
-                def _():
-                    xs[0] = slots(rest + times(tight, o_even)).astype(jnp.bfloat16)
-                    xs[1] = slots(solved).astype(jnp.bfloat16)
-                    hop(0).start()
-                    hop(1).start()
-            emit(solved)
-            for i in range(2):
-                hand_on(i).wait_send()
+                if i == 0:
+                    hand_on().start()
+                rest = rest - times(x_in[i][1], c_even) - times(x_in[i][0], f_even)
+                tight = rest.astype(jnp.bfloat16)
+                solved = kept[i][...] - times(x_in[i][1], far) - times(tight, mixed)
+                if n_unk > 4:
+                    @pl.when(has_next)
+                    def _():
+                        x_out[i][0] = (rest + times(tight, o_even)).astype(jnp.bfloat16)
+                        x_out[i][1] = solved.astype(jnp.bfloat16)
+                        hop(i).start()
+                        if i == 1:
+                            hop_even().start()
+                if i == 0:
+                    acc[...] = solved
+            emit(acc[...], solved)
+            hand_on().wait_send()
 
         for i in range(2):
             pass_on(i).wait_send()
@@ -268,40 +305,50 @@
         def _():
             for i in range(2):
                 hop(i).wait_send()
+            hop_even().wait_send()
 
     @pl.when(is_even)
     def _():
+        @pl.when(jnp.logical_and(quarter < 2, later_pair))
+        def _():
+            near_product()
+
+        @pl.when(jnp.logical_and(quarter == 0, later_pair))
+        def _():
+            far_product()
+
         pl.semaphore_wait(ready, 1)
         for d in range(1, n_freq):
             spread(0, other(d)).start()
         spread(0, me).start()
 
-        @pl.when(later_pair)
-        def _():
-            share(1).start()
-            share(2).start()
-
-        loaded[2].wait()
-
-        @pl.when(later_pair)
-        def _():
-            loaded[3].wait()
-            product(c, c, o, near)
-            loaded[4].wait()
-            product(f, f, o, far)
+        @pl.when(jnp.logical_and(quarter >= 2, later_pair))
+        def _():
+            near_product()
+
+        @pl.when(jnp.logical_and(quarter >= 1, later_pair))
+        def _():
+            far_product()
+
+        @pl.when(first_pair)
+        def _():
+            loaded[2].wait()
 
         for i in range(2):
             pass_on(i).wait_recv()
-        wide, tight = flat(rb_even[...])
-        acc[...] = slots(wide + times(tight, o))
-
-        @pl.when(later_pair)
-        def _():
-            for i in range(2):
-                hand_on(i).wait_recv()
-            acc[...] -= slots(times(flat(xin[1])[1], near) + times(flat(xin[0])[1], far))
-
-        emit(acc[...])
+            wide, tight = ordered(rb_even, i)
+            kept[i][...] = wide + times(tight, o)
+
+        @pl.when(later_pair)
+        def _():
+            for i in range(2):
+                if i == 0:
+                    hand_on().wait_recv()
+                else:
+                    hop_even().wait_recv()
+                kept[i][...] -= times(x_in[i][1], near) + times(x_in[i][0], far)
+
+        emit(acc[...], tail[...])
         share(0).wait_send()
 
         @pl.when(later_pair)
@@ -317,11 +364,13 @@
     freqs = inverse_offset.shape[1] * n_freq
     table = jnp.asarray(transform_matrix(times, freqs, loads))
     bf16 = jnp.bfloat16
+    n_far = max(1, n_freq // 4)
+    rows_near, rows_far = 2 * (n_freq - n_far) * loads, 2 * n_far * loads
     block = pltpu.VMEM((2, rows, rows), bf16)
-    wide = (n_freq, 2 * loads, rows)
+    wide = pltpu.VMEM((n_freq, 2 * loads, rows), bf16)
     dma = pltpu.SemaphoreType.DMA
     return pl.pallas_call(
-        functools.partial(kernel, n_freq, n_unk, min(256, rows)),
+        functools.partial(kernel, n_freq, n_unk, n_far, min(256, rows)),
         out_shape=pltpu.VMEM((2, 1, n_freq * loads, rows), bf16),
         in_specs=[pl.BlockSpec(memory_space=pl.ANY)] * 5,
         out_specs=pl.BlockSpec(memory_space=pltpu.VMEM),
@@ -329,14 +378,12 @@
             pltpu.VMEM(time_samples.shape, bf16),
             pltpu.VMEM(table.shape, bf16),
             *[block] * 9,
-            pltpu.VMEM(wide, bf16),
-            pltpu.VMEM(wide, bf16),
-            pltpu.VMEM(wide, bf16),
-            pltpu.VMEM((2, *wide), bf16),
-            pltpu.VMEM((2, *wide), bf16),
-            pltpu.VMEM(wide, jnp.float32),
+            *[wide] * 3,
+            *[pltpu.VMEM((2, rows_near, rows), bf16), pltpu.VMEM((2, rows_far, rows), bf16)] * 2,
+            pltpu.VMEM((rows_near, rows), jnp.float32),
+            pltpu.VMEM((rows_far, rows), jnp.float32),
             dma((5,)), dma((1,)), dma((4,)), dma((3,)), dma((3,)),
-            dma((2,)), dma((2,)), dma((2,)), dma((2,)), dma((2,)), dma((2,)),
+            dma((2,)), dma((2,)), dma((3,)), dma((3,)), dma((1,)), dma((1,)),
             pltpu.SemaphoreType.REGULAR,
         ],
         compiler_params=pltpu.CompilerParams(collective_id=0, has_side_effects=True),

time: 12.5 us -> 13 us (1.040)
  the two profiles are of different devices: /device:TPU:4 before, /device:TPU:13 now
where the time goes in v2:
time: 13 us; the launch traced here: 12.8 us
  Pallas kernels  12.2 us (94%)
  local copies, waits for them, and re-layouts  0.63 us (5%)
    pallas_call x1, Pallas kernels, per_device(): pl.pallas_call(functools.partial(kernel, n_freq, n_unk, n_far, min(256, r...  12.2 us
    unnamed x1, local copies, waits for them, and re-layouts  0.63 us

profile of v2, /device:TPU:13, one launch (start us, length us, event | category | flops | bytes accessed | tf_op | source)
XLA Modules:
  0.0 12.8 jit_solution(11726648558071055852)
XLA Ops:
  0.0 12.2 %shard_map.55 = bf16[2,1,32,512]{3,2,1,0:T(8,128)(2,1)S(1)} custom-call(bf16[16,4,512]{2,1,0:T(4,128)(2,1)} %ts_hbm.1, bf16[64,128]{1,0:T(8,128)(2,1)} %constant.2.clone.w_hbm, bf16[2,1,512,512]{3,2,1,0:T(8,128)(2,1)} %o_hbm.1, bf16[2,1,512,512]{3,2,1,0:T(8,128)(2,1)} %c_hbm.1, bf16[2,1,512,512]{3,2,1,0:T(8,128)(2,1)} %f_hbm.1), custom_call_target="tpu_custom_call" | custom-call | tf_op jit(solution)/shard_map/pallas_call | solution.py:372
  12.2 0.6 %copy.7 = bf16[2,1,32,512]{3,2,1,0:T(8,128)(2,1)} copy(bf16[2,1,32,512]{3,2,1,0:T(8,128)(2,1)S(1)} %shard_map.55) | data formatting | bytes 131072
